TPU v7x, 32 devices: a whole 2x2x4 slice. The times are simulated.
32 devices in a mesh: row: 4 (over x, core), col: 8 (over z, y).
Axes of the slice: x: 2, y: 2, z: 4, core: 2. Of those that a mesh axis runs over, the one named last changes fastest.
Arguments:
- pair: bfloat16 [768, 768, 512], P('row', 'col'), may hold values from -6 to 6
- w_bias: bfloat16 [512, 96], replicated, may hold values from -0.25 to 0.25
- queries: bfloat16 [768, 1536], P('row', 'col'), may hold values from -360 to 360
- keys: bfloat16 [768, 1536], P('col', 'row'), may hold values from -6 to 6
- values: bfloat16 [768, 1536], P('col', 'row'), may hold values from -6 to 6
- d_out: bfloat16 [768, 1536], P('row', 'col'), may hold values from -6 to 6
Outputs:
- d_pair: bfloat16 [768, 768, 512], P('row', 'col')
- d_wbias: float32 [512, 96], replicated
- d_queries: bfloat16 [768, 1536], P('row', 'col')
- d_keys: bfloat16 [768, 1536], P('col', 'row')
- d_values: bfloat16 [768, 1536], P('col', 'row')
All inputs are finite; a program needn't handle non-finite values.
Results may differ from a plain program's by a relative error of at most 0.0095.
Values may be sent and summed in bfloat16 or wider, within the bound.
A program may use at most 128 MiB of HBM per device.

v0:
```python
import functools

import jax
import jax.numpy as jnp
from jax import lax
from jax.experimental import pallas as pl
from jax.experimental.pallas import tpu as pltpu
from jax.sharding import PartitionSpec as P

H = 96
HD = 16
SCALE = 1.0 / HD**0.5
MESH = pl.DeviceIdType.MESH
VMEM = pltpu.VMEM
DMA = pltpu.SemaphoreType.DMA


def remote(src, dst, send, recv, row, col):
    return pltpu.make_async_remote_copy(
        src_ref=src, dst_ref=dst, send_sem=send, recv_sem=recv,
        device_id=(row, col), device_id_type=MESH,
    )


def greet(nrow, ncol, row, col):
    barrier = pltpu.get_barrier_semaphore()
    for k in range(1, ncol):
        pl.semaphore_signal(
            barrier, inc=1, device_id=(row, lax.rem(col + k, ncol)), device_id_type=MESH
        )
    for k in range(1, nrow):
        pl.semaphore_signal(
            barrier, inc=1, device_id=(lax.rem(row + k, nrow), col), device_id_type=MESH
        )
    pl.semaphore_wait(barrier, ncol + nrow - 2)


def gather_kernel(
    nrow, ncol, wt, pair, q, k_in, v, d, out, qd_all, kv_all,
    qd, kv, qs, qr, fs, fr, ks, kr, own,
):
    row, col = lax.axis_index("row"), lax.axis_index("col")
    inner = 2 if ncol % 2 == 0 else 1
    outer = ncol // inner
    a, b = col // inner, lax.rem(col, inner)
    flip = a * inner + inner - 1 - b
    step, last = pl.program_id(0), pl.num_programs(0) - 1
    steps = out.shape[1]

    def sends():
        copies = []
        for k in range(1, outer):
            to = lax.rem(a + k, outer) * inner + b
            copies.append(remote(qd, qd_all.at[col], qs.at[k], qr.at[k], row, to))
        if inner == 2:
            copies.append(remote(qd, qd_all.at[col], fs.at[0], fr.at[0], row, flip))
        for k in range(1, nrow):
            to = lax.rem(row + k, nrow)
            copies.append(remote(kv, kv_all.at[row], ks.at[k], kr.at[k], to, col))
        copies.append(pltpu.make_async_copy(qd, qd_all.at[col], own.at[0]))
        copies.append(pltpu.make_async_copy(kv, kv_all.at[row], own.at[1]))
        return copies

    def relay(k):
        src = lax.rem(a + outer - k, outer) * inner + b
        return remote(qd_all.at[src], qd_all.at[src], fs.at[k], fr.at[k], row, flip)

    @pl.when(step == 0)
    def _():
        qd[...] = jnp.concatenate([q[...], d[...]], axis=1)
        kv[...] = jnp.concatenate([k_in[...], v[...]], axis=1)
        greet(nrow, ncol, row, col)
        for copy in sends():
            copy.start()

    out[...] = jnp.swapaxes(
        jnp.stack(
            [
                lax.dot_general(
                    wt[...], pair[k], (((1,), (1,)), ((), ())),
                    preferred_element_type=jnp.float32,
                )
                for k in range(steps)
            ]
        ),
        0, 1,
    )

    for k in range(1, outer):

        @pl.when(step == jnp.minimum(last, (last + 1) // 2 + 2 * (k - 1)))
        def _():
            src = lax.rem(a + outer - k, outer) * inner + b
            remote(qd, qd_all.at[src], qs.at[k], qr.at[k], row, col).wait_recv()
            if inner == 2:
                relay(k).start()

    @pl.when(step == last)
    def _():
        if inner == 2:
            for k in range(outer):
                src = lax.rem(a + outer - k, outer) * inner + 1 - b
                remote(qd, qd_all.at[src], fs.at[k], fr.at[k], row, col).wait_recv()
        for k in range(1, nrow):
            src = lax.rem(row + nrow - k, nrow)
            remote(kv, kv_all.at[src], ks.at[k], kr.at[k], row, col).wait_recv()
        copies = sends()
        for copy in copies[:-2]:
            copy.wait_send()
        for copy in copies[-2:]:
            copy.wait()
        if inner == 2:
            for k in range(1, outer):
                relay(k).wait_send()


def gather(nrow, ncol, pair, wt, q, k, v, d, block=8):
    R, C, width = pair.shape
    qd = jax.ShapeDtypeStruct((R, 2 * q.shape[1]), q.dtype)
    kv = jax.ShapeDtypeStruct((C, 2 * k.shape[1]), k.dtype)
    heads = wt.shape[0]
    return pl.pallas_call(
        functools.partial(gather_kernel, nrow, ncol),
        grid=(R // block,),
        out_shape=(
            jax.ShapeDtypeStruct((heads, R, C), jnp.float32),
            jax.ShapeDtypeStruct((ncol,) + qd.shape, qd.dtype),
            jax.ShapeDtypeStruct((nrow,) + kv.shape, kv.dtype),
        ),
        in_specs=[
            pl.BlockSpec((heads, width), lambda i: (0, 0)),
            pl.BlockSpec((block, C, width), lambda i: (i, 0, 0)),
        ]
        + [pl.BlockSpec(memory_space=VMEM)] * 4,
        out_specs=(
            pl.BlockSpec((heads, block, C), lambda i: (0, i, 0)),
            pl.BlockSpec(memory_space=pl.ANY),
            pl.BlockSpec(memory_space=pl.ANY),
        ),
        scratch_shapes=[VMEM(qd.shape, qd.dtype), VMEM(kv.shape, kv.dtype)]
        + [DMA((ncol,))] * 4 + [DMA((nrow,))] * 2 + [DMA((2,))],
        compiler_params=pltpu.CompilerParams(collective_id=0, has_side_effects=True),
    )(wt, pair, q, k, v, d)


def stats_kernel(ncol, st, out, got, back, s1, r1, s2, r2):
    row, col = lax.axis_index("row"), lax.axis_index("col")
    barrier = pltpu.get_barrier_semaphore()
    for k in range(1, ncol):
        pl.semaphore_signal(
            barrier, inc=1, device_id=(row, lax.rem(col + k, ncol)), device_id_type=MESH
        )
    pl.semaphore_wait(barrier, ncol - 1)
    sends = []
    for k in range(1, ncol):
        to = lax.rem(col + k, ncol)
        copy = remote(st.at[to], got.at[k], s1.at[k], r1.at[k], row, to)
        copy.start()
        sends.append(copy)
    got[0] = st[col]
    for k in range(1, ncol):
        remote(st.at[k], got.at[k], s1.at[k], r1.at[k], row, col).wait_recv()
    top = got[0, 0]
    for k in range(1, ncol):
        top = jnp.maximum(top, got[k, 0])
    total = jnp.zeros_like(top)
    upper = jnp.zeros_like(top)
    scales = []
    for k in range(ncol):
        scale = jnp.exp(got[k, 0] - top)
        scales.append(scale)
        total += got[k, 1] * scale
        upper += got[k, 2] * scale
    delta = upper / total
    for k in range(ncol):
        back[k, 0] = scales[k] / total
        back[k, 1] = delta
    for k in range(1, ncol):
        to = lax.rem(col + ncol - k, ncol)
        copy = remote(back.at[k], out.at[col], s2.at[k], r2.at[k], row, to)
        copy.start()
        sends.append(copy)
    out[col] = back[0]
    for k in range(1, ncol):
        src = lax.rem(col + k, ncol)
        remote(back.at[k], out.at[src], s2.at[k], r2.at[k], row, col).wait_recv()
    for copy in sends:
        copy.wait_send()


def stats(ncol, st):
    part = st.shape[2:]
    return pl.pallas_call(
        functools.partial(stats_kernel, ncol),
        out_shape=jax.ShapeDtypeStruct((ncol, 2) + part, jnp.float32),
        in_specs=[pl.BlockSpec(memory_space=VMEM)],
        out_specs=pl.BlockSpec(memory_space=VMEM),
        scratch_shapes=[
            VMEM((ncol, 3) + part, jnp.float32),
            VMEM((ncol, 2) + part, jnp.float32),
        ]
        + [DMA((ncol,))] * 4,
        compiler_params=pltpu.CompilerParams(collective_id=1, has_side_effects=True),
    )(st)


def reduce_kernel(
    nrow, ncol, wb, dq, dkv, wb_out, q_out, k_out, v_out,
    w1, w1sum, w2, w2sum, near, merged, far, kgot,
    ws1, wr1, ws2, wr2, ws3, wr3, ws4, wr4, ns, nr, qs, qr, ks, kr,
):
    row, col = lax.axis_index("row"), lax.axis_index("col")
    greet(nrow, ncol, row, col)
    sends = []

    def go(copy):
        copy.start()
        sends.append(copy)

    for k in range(1, nrow):
        to = lax.rem(row + k, nrow)
        go(remote(wb.at[to], w1.at[k], ws1.at[k], wr1.at[k], to, col))
    inner = 2 if ncol % 2 == 0 else 1
    outer = ncol // inner
    a, b = col // inner, lax.rem(col, inner)
    flip = a * inner + inner - 1 - b
    order = list(range(1, outer)) + [0]
    if inner == 2:
        for k in order:
            to = lax.rem(a + k, outer) * inner + 1 - b
            go(remote(dq.at[to], near.at[k], ns.at[k], nr.at[k], row, flip))
    for k in range(1, nrow):
        to = lax.rem(row + k, nrow)
        go(remote(dkv.at[to], kgot.at[k], ks.at[k], kr.at[k], to, col))
    total = wb[row]
    for k in range(1, nrow):
        remote(wb.at[0], w1.at[k], ws1.at[k], wr1.at[k], row, col).wait_recv()
        total += w1[k]
    w1sum[...] = total

    def pair_sum(k):
        value = dq[lax.rem(a + k, outer) * inner + b].astype(jnp.float32)
        if inner == 2:
            remote(dq.at[0], near.at[k], ns.at[k], nr.at[k], row, col).wait_recv()
            value += near[k].astype(jnp.float32)
        return value

    for k in range(1, ncol):
        to = lax.rem(col + k, ncol)
        go(remote(w1sum.at[to], w2.at[k], ws2.at[k], wr2.at[k], row, to))
    for k in range(1, outer):
        merged[k] = pair_sum(k).astype(merged.dtype)
        to = lax.rem(a + k, outer) * inner + b
        go(remote(merged.at[k], far.at[k], qs.at[k], qr.at[k], row, to))
    part = w1sum[col]
    for k in range(1, ncol):
        remote(w1sum.at[0], w2.at[k], ws2.at[k], wr2.at[k], row, col).wait_recv()
        part += w2[k]
    w2sum[...] = part
    for k in range(1, ncol):
        to = lax.rem(col + k, ncol)
        go(remote(w2sum, wb_out.at[row, col], ws3.at[k], wr3.at[k], row, to))
    wb_out[row, col] = part
    for k in range(1, ncol):
        src = lax.rem(col + ncol - k, ncol)
        remote(w2sum, wb_out.at[row, src], ws3.at[k], wr3.at[k], row, col).wait_recv()
    for k in range(1, nrow):
        to = lax.rem(row + k, nrow)
        go(remote(wb_out.at[row], wb_out.at[row], ws4.at[k], wr4.at[k], to, col))
    grad = dkv[row].astype(jnp.float32)
    for k in range(1, nrow):
        remote(dkv.at[0], kgot.at[k], ks.at[k], kr.at[k], row, col).wait_recv()
        grad += kgot[k].astype(jnp.float32)
    half = k_out.shape[1]
    k_out[...] = grad[:, :half].astype(k_out.dtype)
    v_out[...] = grad[:, half:].astype(v_out.dtype)
    grad = pair_sum(0)
    for k in range(1, outer):
        remote(merged.at[k], far.at[k], qs.at[k], qr.at[k], row, col).wait_recv()
        grad += far[k].astype(jnp.float32)
    q_out[...] = grad.astype(q_out.dtype)
    for k in range(1, nrow):
        src = lax.rem(row + nrow - k, nrow)
        remote(wb_out.at[src], wb_out.at[src], ws4.at[k], wr4.at[k], row, col).wait_recv()
    for copy in sends:
        copy.wait_send()


def reduce_all(nrow, ncol, wb, dq, dkv):
    chunk = wb.shape[2:]
    return pl.pallas_call(
        functools.partial(reduce_kernel, nrow, ncol),
        out_shape=(
            jax.ShapeDtypeStruct(wb.shape, jnp.float32),
            jax.ShapeDtypeStruct(dq.shape[1:], jnp.bfloat16),
            jax.ShapeDtypeStruct((dkv.shape[1], dkv.shape[2] // 2), jnp.bfloat16),
            jax.ShapeDtypeStruct((dkv.shape[1], dkv.shape[2] // 2), jnp.bfloat16),
        ),
        in_specs=[pl.BlockSpec(memory_space=VMEM)] * 3,
        out_specs=[pl.BlockSpec(memory_space=VMEM)] * 4,
        scratch_shapes=[
            VMEM(wb.shape, jnp.float32),
            VMEM((ncol,) + chunk, jnp.float32),
            VMEM((ncol,) + chunk, jnp.float32),
            VMEM(chunk, jnp.float32),
            VMEM(dq.shape, dq.dtype),
            VMEM(dq.shape, dq.dtype),
            VMEM(dq.shape, dq.dtype),
            VMEM(dkv.shape, dkv.dtype),
            DMA((nrow,)), DMA((nrow,)), DMA((ncol,)), DMA((ncol,)),
            DMA((ncol,)), DMA((ncol,)), DMA((nrow,)), DMA((nrow,)),
            DMA((ncol,)), DMA((ncol,)), DMA((ncol,)), DMA((ncol,)), DMA((nrow,)), DMA((nrow,)),
        ],
        compiler_params=pltpu.CompilerParams(collective_id=2, has_side_effects=True),
    )(wb, dq, dkv)


def pair_grad_kernel(wt, pair, ds, d_pair, wb):
    rows = pair.shape[0]
    cols, width = pair.shape[1:]
    by_row = jnp.swapaxes(ds[...].astype(jnp.float32), 0, 1)
    flat = jnp.swapaxes(by_row, 1, 2).astype(jnp.bfloat16).reshape(rows * cols, -1)

    @pl.when(pl.program_id(0) == 0)
    def _():
        wb[...] = jnp.zeros_like(wb)

    d_pair[...] = (
        jnp.dot(flat, wt[...], preferred_element_type=jnp.float32)
        .astype(jnp.bfloat16)
        .reshape(rows, cols, width)
    )
    wb[...] += lax.dot_general(
        flat, pair[...].reshape(rows * cols, width), (((0,), (0,)), ((), ())),
        preferred_element_type=jnp.float32,
    )


def pair_grad(pair, wt, ds, block=16):
    R, C, width = pair.shape
    heads = wt.shape[0]
    return pl.pallas_call(
        pair_grad_kernel,
        grid=(R // block,),
        out_shape=(
            jax.ShapeDtypeStruct(pair.shape, jnp.bfloat16),
            jax.ShapeDtypeStruct((heads, width), jnp.float32),
        ),
        in_specs=[
            pl.BlockSpec((heads, width), lambda i: (0, 0)),
            pl.BlockSpec((block, C, width), lambda i: (i, 0, 0)),
            pl.BlockSpec((heads, block, C), lambda i: (0, i, 0)),
        ],
        out_specs=(
            pl.BlockSpec((block, C, width), lambda i: (i, 0, 0)),
            pl.BlockSpec((heads, width), lambda i: (0, 0)),
        ),
    )(wt, pair, ds)


def on_device(nrow, ncol, pair, w_bias, queries, keys, values, d_out):
    R, C, width = pair.shape
    dcol, drow = queries.shape[1], keys.shape[1]
    wt = w_bias.T
    pair_bias, qd_all, kv_all = gather(
        nrow, ncol, pair, wt,
        queries, keys, values, d_out,
    )
    query_heads = qd_all[:, :, :dcol].transpose(1, 0, 2).reshape(R, H, HD)
    out_heads = qd_all[:, :, dcol:].transpose(1, 0, 2).reshape(R, H, HD)
    key_heads = kv_all[:, :, :drow].transpose(1, 0, 2).reshape(C, H, HD)
    value_heads = kv_all[:, :, drow:].transpose(1, 0, 2).reshape(C, H, HD)
    scores = jnp.einsum(
        "ihd,jhd->hij", query_heads, key_heads, preferred_element_type=jnp.float32
    ) * SCALE + pair_bias
    grad_prob = jnp.einsum(
        "ihd,jhd->hij", out_heads, value_heads, preferred_element_type=jnp.float32
    )
    local_max = jnp.max(scores, axis=-1)
    exp_scores = jnp.exp(scores - local_max[..., None])
    st = jnp.stack(
        [local_max, jnp.sum(exp_scores, axis=-1), jnp.sum(exp_scores * grad_prob, axis=-1)]
    )
    count = H // ncol * R
    lanes = 128 if count % 128 == 0 else R
    st = st.reshape(3, ncol, count // lanes, lanes).transpose(1, 0, 2, 3)
    back = stats(ncol, st).transpose(1, 0, 2, 3).reshape(2, H, R)
    weights = exp_scores * back[0][..., None]
    grad_score = (weights * (grad_prob - back[1][..., None])).astype(jnp.bfloat16)
    weights_low = weights.astype(jnp.bfloat16)
    d_pair, weight_term = pair_grad(pair, wt, grad_score)
    query_term = jnp.einsum(
        "hij,jhd->ihd", grad_score, key_heads, preferred_element_type=jnp.float32
    ) * SCALE
    key_term = jnp.einsum(
        "hij,ihd->jhd", grad_score, query_heads, preferred_element_type=jnp.float32
    ) * SCALE
    value_term = jnp.einsum(
        "hij,ihd->jhd", weights_low, out_heads, preferred_element_type=jnp.float32
    )
    dq = query_term.astype(jnp.bfloat16).reshape(R, ncol, dcol).transpose(1, 0, 2)
    if R * dcol % 2048 == 0:
        dq = dq.reshape(ncol, R * dcol // 128, 128)
    dk = key_term.astype(jnp.bfloat16).reshape(C, nrow, drow).transpose(1, 0, 2)
    dv = value_term.astype(jnp.bfloat16).reshape(C, nrow, drow).transpose(1, 0, 2)
    wb = weight_term.reshape(ncol, H // ncol, nrow, width // nrow).transpose(2, 0, 1, 3)
    wb, q_grad, k_grad, v_grad = reduce_all(nrow, ncol, wb, dq, jnp.concatenate([dk, dv], axis=2))
    d_wbias = wb.transpose(0, 3, 1, 2).reshape(width, H)
    return d_pair, d_wbias, q_grad.reshape(R, dcol), k_grad, v_grad


def solution(mesh):
    return jax.shard_map(
        functools.partial(on_device, mesh.shape["row"], mesh.shape["col"]),
        mesh=mesh,
        in_specs=(
            P("row", "col", None),
            P(),
            P("row", "col"),
            P("col", "row"),
            P("col", "row"),
            P("row", "col"),
        ),
        out_specs=(P("row", "col", None), P(), P("row", "col"), P("col", "row"), P("col", "row")),
        check_vma=False,
    )
```

profile of v0, /device:TPU:0, one launch (start us, length us, event | category | flops | bytes accessed | tf_op | source)
XLA Modules:
  0.0 158.6 jit_solution(3602308892660159538)
XLA Ops:
  0.6 30.4 %shard_map.101 = (f32[96,192,96]{2,1,0:T(8,128)}, bf16[8,192,384]{2,1,0:T(8,128)(2,1)}, bf16[4,96,768]{2,1,0:T(8,128)(2,1)}) custom-call(bf16[96,512]{1,0:T(8,128)(2,1)} %bitcast.71, bf16[192,96,512]{2,1,0:T(8,128)(2,1)} %pair.3, bf16[192,192]{1,0:T(8,128)(2,1)} %q.1, bf16[96,384]{1,0:T(8,128)(2,1)} %k_in.1, bf16[96,384]{1,0:T(8,128)(2,1)} %v.1, ...), custom_call_target="tpu_custom_call" | custom-call | tf_op jit(solution)/shard_map/pallas_call | solution.py:122
  31.1 1.8 %slice_bitcast_fusion.1 = (bf16[192,8,192]{2,0,1:T(8,128)(2,1)S(1)}, bf16[192,8,192]{2,0,1:T(8,128)(2,1)S(1)}) fusion(bf16[8,192,384]{2,1,0:T(8,128)(2,1)} %get-tuple-element.14), kind=kLoop, calls=%fused_computation.14 | loop fusion | bytes 2359296 | tf_op jit(solution)/shard_map/transpose | solution.py:369
  32.8 0.3 copy.15
  33.2 1.1 slice_bitcast_fusion.3
  34.3 0.2 copy.16
  34.5 9.3 %fusion.7 = (f32[96,192]{1,0:T(8,128)S(1)}, f32[96,192,96]{2,1,0:T(8,128)}) fusion(f32[96,192,96]{2,1,0:T(8,128)} %get-tuple-element.16, bf16[192,96,16]{0,2,1:T(8,128)(2,1)S(1)} %bitcast.55, bf16[96,96,16]{0,2,1:T(8,128)(2,1)S(1)} %bitcast.59), kind=kOutput, calls=%fused_computation.22 | convolution fusion | flops 61913088 | bytes 15114240 | tf_op jit(solution)/shard_map/ihd,jhd->hij/dot_general | solution.py:373
  43.9 0.2 copy.19
  44.1 0.3 copy.18
  44.5 13.6 %fusion = (f32[96,192]{1,0:T(8,128)S(1)}, f32[96,192]{1,0:T(8,128)S(1)}, f32[96,192,96]{2,1,0:T(8,128)}) fusion(f32[96,192,96]{2,1,0:T(8,128)} %get-tuple-element.32, f32[96,192]{1,0:T(8,128)S(1)} %get-tuple-element.31, bf16[192,96,16]{0,2,1:T(8,128)(2,1)S(1)} %bitcast.57, bf16[96,96,16]{0,2,1:T(8,128)(2,1)S(1)} %bitcast.64), kind=kOutput, calls=%fused_computation.5 | convolution fusion | flops 63664128 | bytes 15261696 | tf_op jit(solution)/shard_map/ihd,jhd->hij/dot_general | solution.py:376
  58.1 0.1 stack.14
  58.2 0.7 maximum_bitcast_fusion.st
  59.0 16.7 %shard_map.102 = f32[8,2,18,128]{3,2,1,0:T(8,128)} custom-call(f32[8,3,18,128]{3,2,1,0:T(8,128)} %maximum_bitcast_fusion.st), custom_call_target="tpu_custom_call" | custom-call | tf_op jit(solution)/shard_map/pallas_call | solution.py:193
  75.7 1.0 fusion.6
  76.7 8.4 %fusion.4 = bf16[96,16,96]{2,1,0:T(8,128)(2,1)S(1)} fusion(bf16[192,96,16]{0,2,1:T(8,128)(2,1)S(1)} %bitcast.58, f32[96,192,96]{2,1,0:T(8,128)} %get-tuple-element.32, f32[96,192]{1,0:T(8,128)S(1)} %mul.39, f32[96,192]{1,0:T(8,128)S(1)} %get-tuple-element.31), kind=kOutput, calls=%fused_computation.11 | convolution fusion | flops 62078976 | bytes 8110080 | tf_op jit(solution)/shard_map/hij,ihd->jhd/dot_general | solution.py:398
  85.1 0.2 copy.28
  85.4 10.5 %multiply_convert_fusion.ds = bf16[96,192,96]{2,1,0:T(8,128)(2,1)S(1)} fusion(f32[96,192,96]{2,1,0:T(8,128)} %get-tuple-element.33, f32[96,192,96]{2,1,0:T(8,128)} %get-tuple-element.32, f32[96,192]{1,0:T(8,128)S(1)} %sub.20, f32[96,192]{1,0:T(8,128)S(1)} %mul.39, f32[96,192]{1,0:T(8,128)S(1)} %get-tuple-element.31), kind=kLoop, calls=%fused_computation | loop fusion | flops 8847360 | bytes 17915904 | tf_op jit(solution)/shard_map/convert_element_type | solution.py:389
  95.9 2.1 %copy-done = bf16[96,192,96]{2,1,0:T(8,128)(2,1)} copy-done((bf16[96,192,96]{2,1,0:T(8,128)(2,1)}, bf16[96,192,96]{2,1,0:T(8,128)(2,1)S(1)}, u32[]{:S(2)}) %copy-start) | copy-done | bytes 3538968
  98.0 1.4 fusion.5
  99.4 0.2 copy.27
  99.6 0.9 pad_maximum_fusion.dkv
  100.5 4.9 %multiply_convert_fusion.3 = bf16[96,16,192]{2,1,0:T(8,128)(2,1)S(1)} fusion(bf16[96,96,16]{0,2,1:T(8,128)(2,1)S(1)} %bitcast.60, bf16[96,192,96]{2,1,0:T(8,128)(2,1)} %copy-done), kind=kOutput, calls=%fused_computation.9 | convolution fusion | flops 57212928 | bytes 4423680 | tf_op jit(solution)/shard_map/hij,jhd->ihd/dot_general | solution.py:392
  105.4 0.4 copy.26
  105.7 1.8 %reshape.64.dq = bf16[8,288,128]{2,1,0:T(8,128)(2,1)} reshape(bf16[8,192,192]{2,1,0:T(8,128)(2,1)S(1)} %bitcast.61) | data formatting | bytes 1179648 | tf_op jit(solution)/shard_map/reshape | solution.py:403
  107.5 20.0 %shard_map.103 = (bf16[192,96,512]{2,1,0:T(8,128)(2,1)}, f32[96,512]{1,0:T(8,128)}) custom-call(bf16[96,512]{1,0:T(8,128)(2,1)} %bitcast.72, bf16[192,96,512]{2,1,0:T(8,128)(2,1)} %pair.3, bf16[96,192,96]{2,1,0:T(8,128)(2,1)} %copy-done), custom_call_target="tpu_custom_call" | custom-call | tf_op jit(solution)/shard_map/pallas_call | solution.py:342
  127.5 1.0 reshape.62
  128.5 0.7 copy.35
  129.2 22.9 %shard_map.104 = (f32[4,8,12,128]{3,2,1,0:T(8,128)}, bf16[288,128]{1,0:T(8,128)(2,1)}, bf16[96,384]{1,0:T(8,128)(2,1)}, bf16[96,384]{1,0:T(8,128)(2,1)}) custom-call(f32[4,8,12,128]{3,2,1,0:T(8,128)} %bitcast.68, bf16[8,288,128]{2,1,0:T(8,128)(2,1)} %reshape.64.dq, bf16[4,96,768]{2,1,0:T(8,128)(2,1)} %pad_maximum_fusion.dkv), custom_call_target="tpu_custom_call" | custom-call | tf_op jit(solution)/shard_map/pallas_call | solution.py:291
  152.2 1.1 copy.29
  153.2 0.7 copy.36
  153.9 1.6 %reshape.68 = bf16[192,192]{1,0:T(8,128)(2,1)} reshape(bf16[288,128]{1,0:T(8,128)(2,1)} %get-tuple-element.20) | data formatting | bytes 147456 | tf_op jit(solution)/shard_map/reshape | solution.py:409
  155.6 1.5 copy.39
  157.1 1.5 copy.40
  (5 shorter events, 0.4 us)
Async XLA Ops:
  95.9 2.1 %copy-start = (bf16[96,192,96]{2,1,0:T(8,128)(2,1)}, bf16[96,192,96]{2,1,0:T(8,128)(2,1)S(1)}, u32[]{:S(2)}) copy-start(bf16[96,192,96]{2,1,0:T(8,128)(2,1)S(1)} %multiply_convert_fusion.ds) | copy-start | bytes 10616836
where the time goes:
time: 160 us; the launch traced here: 159 us
  Pallas kernels  90 us (56%)
  matrix products  37.4 us (23%)
  local copies, waits for them, and re-layouts  18.3 us (11%)
  other arithmetic  12.1 us (8%)
    pallas_call x1, Pallas kernels, gather(): pl.pallas_call(functools.partial(gather_kernel, nrow, ncol), grid=(R // b...  30.4 us
    pallas_call x1, Pallas kernels, reduce_all(): pl.pallas_call(functools.partial(reduce_kernel, nrow, ncol), out_shape=(j...  22.9 us
    pallas_call x1, Pallas kernels, pair_grad(): pl.pallas_call(pair_grad_kernel, grid=(R // block,), out_shape=(jax.Shape...  20 us
    pallas_call x1, Pallas kernels, stats(): pl.pallas_call(functools.partial(stats_kernel, ncol), out_shape=jax.Shape...  16.7 us
    dot_general x1, matrix products, on_device(): jnp.einsum('ihd,jhd->hij', out_heads, value_heads, preferred_element_type...  13.6 us
    convert_element_type x1, other arithmetic, on_device(): (weights * (grad_prob - back[1][..., None])).astype(jnp.bfloat16)  10.5 us
    dot_general x1, matrix products, on_device(): jnp.einsum('ihd,jhd->hij', query_heads, key_heads, preferred_element_type...  9.26 us
    dot_general x1, matrix products, on_device(): jnp.einsum('hij,ihd->jhd', weights_low, out_heads, preferred_element_type...  8.39 us

commit v1 on v0

v1 whole, which is shorter than its diff:
```python
import functools

import jax
import jax.numpy as jnp
from jax import lax
from jax.experimental import pallas as pl
from jax.experimental.pallas import tpu as pltpu
from jax.sharding import PartitionSpec as P

HD = 16
SCALE = 1.0 / HD**0.5
LANES = 128
STEP = 16
SLOTS = 2
MESH = pl.DeviceIdType.MESH
VMEM = pltpu.VMEM
DMA = pltpu.SemaphoreType.DMA
F32 = jnp.float32
BF16 = jnp.bfloat16


def remote(src, dst, send, recv, row, col):
    return pltpu.make_async_remote_copy(
        src_ref=src, dst_ref=dst, send_sem=send, recv_sem=recv,
        device_id=(row, col), device_id_type=MESH,
    )


def greet(nrow, ncol, row, col):
    barrier = pltpu.get_barrier_semaphore()
    for k in range(1, ncol):
        pl.semaphore_signal(
            barrier, inc=1, device_id=(row, lax.rem(col + k, ncol)), device_id_type=MESH
        )
    for k in range(1, nrow):
        pl.semaphore_signal(
            barrier, inc=1, device_id=(lax.rem(row + k, nrow), col), device_id_type=MESH
        )
    pl.semaphore_wait(barrier, ncol + nrow - 2)


def dot(a, b):
    return jnp.dot(a, b, preferred_element_type=F32)


def dot_nt(a, b):
    return lax.dot_general(a, b, (((1,), (1,)), ((), ())), preferred_element_type=F32)


def main_kernel(
    nrow, ncol, wt, pair, q, k_in, v, d,
    f_out, wb_out, q_out, k_out, v_out,
    pv, bias, e_buf, g_buf, qd, kv, qd_all, kv_all, qt, dt, kt, vt,
    st, got, back, bk, dq, dq_got, dkv, dkv_got,
    acc, wb, w1, w1sum, w2, w2sum, f_st,
    psem, qs, qr, fs, fr, ks, kr, s1, r1, s2, r2, gs, gr, hs, hr_sem,
    ws1, wr1, ws2, wr2, ws3, wr3, ws4, wr4, fsem,
):
    row, col = lax.axis_index("row"), lax.axis_index("col")
    R, C, W = pair.shape
    H = wt.shape[0]
    Cp = pv.shape[1]
    hb, hr = H // ncol, H // nrow
    dcol, drow = hb * HD, hr * HD
    wr = W // nrow
    chunks = R // STEP
    inner = 2 if ncol % 2 == 0 else 1
    outer = ncol // inner
    a, b_in = col // inner, lax.rem(col, inner)
    flip = a * inner + inner - 1 - b_in

    def load(t):
        rows = pl.ds(t * STEP, STEP)
        return pltpu.make_async_copy(pair.at[rows], pv.at[rows, pl.ds(0, C)], psem.at[t])

    @pl.loop(0, chunks)
    def _(t):
        load(t).start()

    qd_own = jnp.concatenate([q[...], d[...]], axis=1)
    kv_own = jnp.concatenate([k_in[...], v[...]], axis=1)
    qd[...] = qd_own
    kv[...] = kv_own
    qd_all[col] = qd_own
    kv_all[row] = kv_own
    greet(nrow, ncol, row, col)

    def relay(k):
        src = lax.rem(a + outer - k, outer) * inner + b_in
        return remote(qd_all.at[src], qd_all.at[src], fs.at[k], fr.at[k], row, flip)

    first = []
    for k in range(1, outer):
        to = lax.rem(a + k, outer) * inner + b_in
        first.append(remote(qd, qd_all.at[col], qs.at[k], qr.at[k], row, to))
    if inner == 2:
        first.append(remote(qd, qd_all.at[col], fs.at[0], fr.at[0], row, flip))
    for k in range(1, nrow):
        to = lax.rem(row + k, nrow)
        first.append(remote(kv, kv_all.at[row], ks.at[k], kr.at[k], to, col))
    for copy in first:
        copy.start()
    if Cp > C:
        pv[:, C:, :] = jnp.zeros((R, Cp - C, W), BF16)

    @pl.loop(0, chunks)
    def _(t):
        load(t).wait()
        for u in range(0, STEP, 2):
            i = t * STEP + u
            r = dot_nt(wt[...], pv[pl.ds(i, 2)].reshape(2 * Cp, W))
            bias[pl.ds(i, H, stride=R), :] = r[:, :Cp]
            bias[pl.ds(i + 1, H, stride=R), :] = r[:, Cp:]
        for k in range(1, outer):

            @pl.when(t == min(chunks - 1, chunks // 2 + 2 * (k - 1)))
            def _():
                src = lax.rem(a + outer - k, outer) * inner + b_in
                remote(qd, qd_all.at[src], qs.at[k], qr.at[k], row, col).wait_recv()
                if inner == 2:
                    relay(k).start()

    for k in range(1, nrow):
        src = lax.rem(row + nrow - k, nrow)
        remote(kv, kv_all.at[src], ks.at[k], kr.at[k], row, col).wait_recv()

    @pl.loop(0, nrow)
    def _(r):
        x = kv_all[r].T
        kt[pl.ds(r * hr, hr)] = x[:drow].reshape(hr, HD, C)
        vt[pl.ds(r * hr, hr)] = x[drow:].reshape(hr, HD, C)

    if inner == 2:
        for k in range(outer):
            src = lax.rem(a + outer - k, outer) * inner + 1 - b_in
            remote(qd, qd_all.at[src], fs.at[k], fr.at[k], row, col).wait_recv()

    lag = ncol // 2

    def combine():
        for k in range(1, ncol):
            src = lax.rem(col + k, ncol)
            remote(st.at[src], got.at[src], s1.at[src], r1.at[src], row, col).wait_recv()
        got[col] = st[col]
        top = got[0, 0]
        for k in range(1, ncol):
            top = jnp.maximum(top, got[k, 0])
        total = jnp.zeros_like(top)
        upper = jnp.zeros_like(top)
        for k in range(ncol):
            scale = jnp.exp(got[k, 0] - top)
            total += got[k, 1] * scale
            upper += got[k, 2] * scale
        delta = upper / total
        for k in range(ncol):
            back[k, 0] = jnp.exp(got[k, 0] - top) / total
            back[k, 1] = delta
        bk[col] = back[col]
        for k in range(1, ncol):
            to = lax.rem(col + k, ncol)
            remote(back.at[to], bk.at[col], s2.at[to], r2.at[col], row, to).start()

    @pl.loop(0, ncol)
    def _(b):
        x = qd_all[b].T
        qt[pl.ds(b * hb, hb)] = (x[:dcol] * jnp.asarray(SCALE, BF16)).reshape(hb, HD, R)
        dt[pl.ds(b * hb, hb)] = x[dcol:].reshape(hb, HD, R)
        heads = pl.ds(b * hb, hb)
        kb = kt[heads].reshape(dcol, C).T
        vb = vt[heads].reshape(dcol, C).T
        qb = qt[heads].reshape(dcol, R)
        db = dt[heads].reshape(dcol, R)
        owner = lax.broadcasted_iota(jnp.int32, (C, dcol), 1) // HD
        zero = jnp.zeros((C, dcol), BF16)
        for t in range(hb):
            h = b * hb + t
            term = bias[pl.ds(pl.multiple_of(h * R, 8), R), :].T[:C]
            s = dot(jnp.where(owner == t, kb, zero), qb) + term
            g = dot(jnp.where(owner == t, vb, zero), db)
            top = jnp.max(s, axis=0, keepdims=True)
            e = jnp.exp(s - top)
            e_buf[h] = e
            g_buf[h] = g
            st[b, 0, pl.ds(t, 1)] = top
            st[b, 1, pl.ds(t, 1)] = jnp.sum(e, axis=0, keepdims=True)
            st[b, 2, pl.ds(t, 1)] = jnp.sum(e * g, axis=0, keepdims=True)

        @pl.when(col != b)
        def _():
            remote(st.at[b], got.at[col], s1.at[b], r1.at[col], row, b).start()

        @pl.when(col == b - lag)
        def _():
            combine()

    per = hr // hb if hr % hb == 0 else 0

    def send_dkv(r):
        remote(dkv.at[r], dkv_got.at[row], gs.at[r], gr.at[row], r, col).start()

    @pl.loop(0, ncol)
    def _(b):
        @pl.when(col == ncol - lag + b)
        def _():
            combine()

        @pl.when(col != b)
        def _():
            remote(back.at[b], bk.at[b], s2.at[b], r2.at[b], row, col).wait_recv()

        for t in range(hb):
            h = b * hb + t
            r = h // hr
            w = e_buf[h] * bk[b, 0, pl.ds(t, 1)]
            ds = (w * (g_buf[h] - bk[b, 1, pl.ds(t, 1)])).astype(BF16)
            low = w.astype(BF16)
            dq[b, t] = (dot(kt[h], ds) * SCALE).astype(BF16)
            dkv[r, 0, lax.rem(h, hr)] = dot_nt(qt[h], ds).astype(BF16)
            dkv[r, 1, lax.rem(h, hr)] = dot_nt(dt[h], low).astype(BF16)
            bias[pl.ds(pl.multiple_of(h * R, 8), R), pl.ds(0, C)] = ds.astype(F32).T

        @pl.when(col != b)
        def _():
            remote(dq.at[b], dq_got.at[col], hs.at[b], hr_sem.at[col], row, b).start()

        if per:
            done = b // per

            @pl.when(jnp.logical_and(lax.rem(b, per) == per - 1, row != done))
            def _():
                send_dkv(done)

    if not per:
        for k in range(1, nrow):
            send_dkv(lax.rem(row + k, nrow))

    acc[...] = jnp.zeros_like(acc)

    def rows_of(i):
        return bias[pl.ds(i, H, stride=R), :]

    @pl.loop(0, chunks)
    def _(t):
        total = acc[...]
        for u in range(0, STEP, 2):
            i = t * STEP + u
            lhs = jnp.concatenate(
                [rows_of(i).astype(BF16), rows_of(i + 1).astype(BF16)], axis=1
            )
            total = total + dot(lhs, pv[pl.ds(i, 2)].reshape(2 * Cp, W))
        acc[...] = total

    for r in range(nrow):
        for b in range(ncol):
            wb[r, b] = acc[b * hb:(b + 1) * hb, r * wr:(r + 1) * wr]

    def put(t, slot):
        return pltpu.make_async_copy(
            f_st.at[slot], f_out.at[pl.ds(t * STEP, STEP)], fsem.at[slot]
        )

    def flat(lo, hi):
        @pl.loop(lo, hi)
        def _(t):
            slot = lax.rem(t, SLOTS)

            @pl.when(t >= SLOTS)
            def _():
                put(t - SLOTS, slot).wait()

            for u in range(STEP):
                f_st[slot, u] = rows_of(t * STEP + u).T[:C].astype(BF16)
            put(t, slot).start()

    cuts = [0, chunks // 4, (2 * chunks) // 3, chunks - chunks // 8, chunks]

    for k in range(1, nrow):
        to = lax.rem(row + k, nrow)
        remote(wb.at[to], w1.at[k], ws1.at[k], wr1.at[k], to, col).start()
    flat(cuts[0], cuts[1])
    total = wb[row]
    for k in range(1, nrow):
        remote(wb.at[0], w1.at[k], ws1.at[k], wr1.at[k], row, col).wait_recv()
        total += w1[k]
    w1sum[...] = total
    for k in range(1, ncol):
        to = lax.rem(col + k, ncol)
        remote(w1sum.at[to], w2.at[k], ws2.at[k], wr2.at[k], row, to).start()
    flat(cuts[1], cuts[2])
    part = w1sum[col]
    for k in range(1, ncol):
        remote(w1sum.at[0], w2.at[k], ws2.at[k], wr2.at[k], row, col).wait_recv()
        part += w2[k]
    w2sum[...] = part
    wb_out[row, col] = part
    for k in range(1, ncol):
        to = lax.rem(col + k, ncol)
        remote(w2sum, wb_out.at[row, col], ws3.at[k], wr3.at[k], row, to).start()
    flat(cuts[2], cuts[3])

    grad = dkv[row].astype(F32)
    for k in range(1, nrow):
        src = lax.rem(row + k, nrow)
        remote(dkv.at[0], dkv_got.at[src], gs.at[0], gr.at[src], row, col).wait_recv()
        grad += dkv_got[src].astype(F32)
    k_out[...] = grad[0].reshape(drow, C).T.astype(BF16)
    v_out[...] = grad[1].reshape(drow, C).T.astype(BF16)
    total_q = dq[col].astype(F32)
    for k in range(1, ncol):
        src = lax.rem(col + k, ncol)
        remote(dq.at[0], dq_got.at[src], hs.at[0], hr_sem.at[src], row, col).wait_recv()
        total_q += dq_got[src].astype(F32)
    q_out[...] = total_q.reshape(dcol, R).T.astype(BF16)

    for k in range(1, ncol):
        src = lax.rem(col + ncol - k, ncol)
        remote(w2sum, wb_out.at[row, src], ws3.at[k], wr3.at[k], row, col).wait_recv()
    for k in range(1, nrow):
        to = lax.rem(row + k, nrow)
        remote(wb_out.at[row], wb_out.at[row], ws4.at[k], wr4.at[k], to, col).start()
    flat(cuts[3], cuts[4])
    for k in range(1, nrow):
        src = lax.rem(row + nrow - k, nrow)
        remote(wb_out.at[src], wb_out.at[src], ws4.at[k], wr4.at[k], row, col).wait_recv()

    for t in range(max(0, chunks - SLOTS), chunks):
        put(t, t % SLOTS).wait()
    for copy in first:
        copy.wait_send()
    if inner == 2:
        for k in range(1, outer):
            relay(k).wait_send()
    for k in range(1, ncol):
        to = lax.rem(col + k, ncol)
        remote(st.at[to], got.at[col], s1.at[to], r1.at[col], row, to).wait_send()
        remote(back.at[to], bk.at[col], s2.at[to], r2.at[col], row, to).wait_send()
        remote(dq.at[to], dq_got.at[col], hs.at[to], hr_sem.at[col], row, to).wait_send()
        remote(w1sum.at[to], w2.at[k], ws2.at[k], wr2.at[k], row, to).wait_send()
        remote(w2sum, wb_out.at[row, col], ws3.at[k], wr3.at[k], row, to).wait_send()
    for k in range(1, nrow):
        to = lax.rem(row + k, nrow)
        remote(dkv.at[to], dkv_got.at[row], gs.at[to], gr.at[row], to, col).wait_send()
        remote(wb.at[to], w1.at[k], ws1.at[k], wr1.at[k], to, col).wait_send()
        remote(wb_out.at[row], wb_out.at[row], ws4.at[k], wr4.at[k], to, col).wait_send()


def main(nrow, ncol, wt, pair, q, k, v, d):
    R, C, W = pair.shape
    H = wt.shape[0]
    hb, hr = H // ncol, H // nrow
    dcol, drow = q.shape[1], k.shape[1]
    Cp = -(-C // LANES) * LANES
    wr = W // nrow
    shape = jax.ShapeDtypeStruct
    return pl.pallas_call(
        functools.partial(main_kernel, nrow, ncol),
        out_shape=(
            shape((R, C, H), BF16),
            shape((nrow, ncol, hb, wr), F32),
            shape((R, dcol), BF16),
            shape((C, drow), BF16),
            shape((C, drow), BF16),
        ),
        in_specs=[pl.BlockSpec(memory_space=VMEM), pl.BlockSpec(memory_space=pl.ANY)]
        + [pl.BlockSpec(memory_space=VMEM)] * 4,
        out_specs=[pl.BlockSpec(memory_space=pl.ANY)] + [pl.BlockSpec(memory_space=VMEM)] * 4,
        scratch_shapes=[
            VMEM((R, Cp, W), BF16),
            VMEM((H * R, Cp), F32),
            VMEM((H, C, R), F32),
            VMEM((H, C, R), F32),
            VMEM((R, 2 * dcol), BF16),
            VMEM((C, 2 * drow), BF16),
            VMEM((ncol, R, 2 * dcol), BF16),
            VMEM((nrow, C, 2 * drow), BF16),
            VMEM((H, HD, R), BF16),
            VMEM((H, HD, R), BF16),
            VMEM((H, HD, C), BF16),
            VMEM((H, HD, C), BF16),
            VMEM((ncol, 3, hb, R), F32),
            VMEM((ncol, 3, hb, R), F32),
            VMEM((ncol, 2, hb, R), F32),
            VMEM((ncol, 2, hb, R), F32),
            VMEM((ncol, hb, HD, R), BF16),
            VMEM((ncol, hb, HD, R), BF16),
            VMEM((nrow, 2, hr, HD, C), BF16),
            VMEM((nrow, 2, hr, HD, C), BF16),
            VMEM((H, W), F32),
            VMEM((nrow, ncol, hb, wr), F32),
            VMEM((nrow, ncol, hb, wr), F32),
            VMEM((ncol, hb, wr), F32),
            VMEM((ncol, hb, wr), F32),
            VMEM((hb, wr), F32),
            VMEM((SLOTS, STEP, C, H), BF16),
            DMA((R // STEP,)),
            DMA((ncol,)), DMA((ncol,)), DMA((ncol,)), DMA((ncol,)),
            DMA((nrow,)), DMA((nrow,)),
            DMA((ncol,)), DMA((ncol,)), DMA((ncol,)), DMA((ncol,)),
            DMA((nrow,)), DMA((nrow,)), DMA((ncol,)), DMA((ncol,)),
            DMA((nrow,)), DMA((nrow,)), DMA((ncol,)), DMA((ncol,)),
            DMA((ncol,)), DMA((ncol,)), DMA((nrow,)), DMA((nrow,)),
            DMA((SLOTS,)),
        ],
        compiler_params=pltpu.CompilerParams(
            collective_id=0, has_side_effects=True, vmem_limit_bytes=67043328
        ),
    )(wt, pair, q, k, v, d)


def finish_kernel(f, wt, wb, q, k, v, d_pair, wo, qo, ko, vo):
    rows, C, H = f.shape
    d_pair[...] = dot(f[...].reshape(rows * C, H), wt[...]).astype(BF16).reshape(d_pair.shape)

    @pl.when(pl.program_id(0) == 0)
    def _():
        qo[...] = q[...]
        ko[...] = k[...]
        vo[...] = v[...]
        nrow, wr = wb.shape[0], wb.shape[3]
        for r in range(nrow):
            wo[:, r * wr:(r + 1) * wr] = wb[r].reshape(H, wr)


def finish(f, wt, wb, q, k, v, block=16):
    R, C, H = f.shape
    W = wt.shape[1]

    def whole(x):
        return pl.BlockSpec(x.shape, lambda i: (0,) * len(x.shape))

    return pl.pallas_call(
        finish_kernel,
        grid=(R // block,),
        out_shape=(
            jax.ShapeDtypeStruct((R, C, W), BF16),
            jax.ShapeDtypeStruct((H, W), F32),
            jax.ShapeDtypeStruct(q.shape, BF16),
            jax.ShapeDtypeStruct(k.shape, BF16),
            jax.ShapeDtypeStruct(v.shape, BF16),
        ),
        in_specs=[pl.BlockSpec((block, C, H), lambda i: (i, 0, 0))]
        + [whole(x) for x in (wt, wb, q, k, v)],
        out_specs=(
            pl.BlockSpec((block, C, W), lambda i: (i, 0, 0)),
            pl.BlockSpec((H, W), lambda i: (0, 0)),
            whole(q), whole(k), whole(v),
        ),
    )(f, wt, wb, q, k, v)


def on_device(nrow, ncol, pair, w_bias, queries, keys, values, d_out):
    wt = w_bias.T
    f, wb, q, k, v = main(nrow, ncol, wt, pair, queries, keys, values, d_out)
    d_pair, d_wbias, d_queries, d_keys, d_values = finish(f, wt, wb, q, k, v)
    return d_pair, d_wbias.T, d_queries, d_keys, d_values


def solution(mesh):
    return jax.shard_map(
        functools.partial(on_device, mesh.shape["row"], mesh.shape["col"]),
        mesh=mesh,
        in_specs=(
            P("row", "col", None),
            P(),
            P("row", "col"),
            P("col", "row"),
            P("col", "row"),
            P("row", "col"),
        ),
        out_specs=(P("row", "col", None), P(), P("row", "col"), P("col", "row"), P("col", "row")),
        check_vma=False,
    )
```

time: 160 us -> 96.8 us (0.60)
  matrix products: 37.4 us -> 0 us
  local copies, waits for them, and re-layouts: 18.3 us -> 0 us
  other arithmetic: 12.1 us -> 0 us
  Pallas kernels: 90 us -> 95.7 us
    dot_general x5 -> x0, matrix products: 37.4 us -> none  [the longest x1 13.6 us: on_device(): jnp.einsum('ihd,jhd->hij', out_heads, value_heads, preferred_element_type...]
    convert_element_type x1 -> x0, other arithmetic: 10.5 us -> none  [on_device(): (weights * (grad_prob - back[1][..., None])).astype(jnp.bfloat16)]
    reshape x7 -> x0, local copies, waits for them, and re-layouts: 5.92 us -> none  [the longest x1 1.77 us: on_device(): dq = dq.reshape(ncol, R * dcol // 128, 128)]
    unnamed x5 -> x0, local copies, waits for them, and re-layouts: 5.85 us -> none
    pallas_call x4 -> x2, Pallas kernels: 90 us -> 95.7 us  [the longest x1 81.8 us: main(): pl.pallas_call(functools.partial(main_kernel, nrow, ncol), out_shape=(sha...]
    transpose x7 -> x0, local copies, waits for them, and re-layouts: 5.08 us -> none  [the longest x2 2.09 us: on_device(): query_heads = qd_all[:, :, :dcol].transpose(1, 0, 2).reshape(R, H, HD)]
where the time goes in v1:
time: 96.8 us; the launch traced here: 96.3 us
  Pallas kernels  95.7 us (99%)
    pallas_call x1, Pallas kernels, main(): pl.pallas_call(functools.partial(main_kernel, nrow, ncol), out_shape=(sha...  81.8 us
    pallas_call x1, Pallas kernels, finish(): pl.pallas_call(finish_kernel, grid=(R // block,), out_shape=(jax.ShapeDty...  13.9 us

profile of v1, /device:TPU:0, one launch (start us, length us, event | category | flops | bytes accessed | tf_op | source)
XLA Modules:
  0.0 96.3 jit_solution(594795560521421030)
XLA Ops:
  0.6 81.8 %shard_map.101 = (bf16[192,96,96]{2,1,0:T(8,128)(2,1)}, f32[4,8,12,128]{3,2,1,0:T(8,128)}, bf16[192,192]{1,0:T(8,128)(2,1)}, bf16[96,384]{1,0:T(8,128)(2,1)}, bf16[96,384]{1,0:T(8,128)(2,1)}) custom-call(bf16[96,512]{1,0:T(8,128)(2,1)} %bitcast.2, bf16[192,96,512]{2,1,0:T(8,128)(2,1)} %pair.1, bf16[192,192]{1,0:T(8,128)(2,1)} %q.1, bf16[96,384]{1,0:T(8,128)(2,1)} %k_in.1, ...), custom_call_target="tpu_custom_call" | custom-call | tf_op jit(solution)/shard_map/pallas_call | solution.py:355
  82.5 13.9 %shard_map.102 = (bf16[192,96,512]{2,1,0:T(8,128)(2,1)}, f32[96,512]{1,0:T(8,128)}, bf16[192,192]{1,0:T(8,128)(2,1)}, bf16[96,384]{1,0:T(8,128)(2,1)}, bf16[96,384]{1,0:T(8,128)(2,1)}) custom-call(bf16[192,96,96]{2,1,0:T(8,128)(2,1)} %get-tuple-element.15.f, bf16[96,512]{1,0:T(8,128)(2,1)} %bitcast.3, f32[4,8,12,128]{3,2,1,0:T(8,128)} %get-tuple-element.16.wb, ...), custom_call_target="tpu_custom_call" | custom-call | tf_op jit(solution)/shard_map/pallas_call | solution.py:431

commit v2 on v1

--- a/solution.py
+++ b/solution.py
@@ -12,6 +12,7 @@
 LANES = 128
 STEP = 16
 SLOTS = 2
+HOP = 4
 MESH = pl.DeviceIdType.MESH
 VMEM = pltpu.VMEM
 DMA = pltpu.SemaphoreType.DMA
@@ -24,6 +25,15 @@
         src_ref=src, dst_ref=dst, send_sem=send, recv_sem=recv,
         device_id=(row, col), device_id_type=MESH,
     )
+
+
+def split(n):
+    return (2, n // 2) if n % 2 == 0 else (1, n)
+
+
+def folds(R, hb):
+    half = R % LANES
+    return R == LANES + half and 2 * half == LANES and hb % 2 == 0, half
 
 
 def greet(nrow, ncol, row, col):
@@ -51,9 +61,10 @@
     nrow, ncol, wt, pair, q, k_in, v, d,
     f_out, wb_out, q_out, k_out, v_out,
     pv, bias, e_buf, g_buf, qd, kv, qd_all, kv_all, qt, dt, kt, vt,
-    st, got, back, bk, dq, dq_got, dkv, dkv_got,
+    st, got, back, bk, dq, dq_near, dq_far, dkv, dkv_near, dkv_far,
     acc, wb, w1, w1sum, w2, w2sum, f_st,
-    psem, qs, qr, fs, fr, ks, kr, s1, r1, s2, r2, gs, gr, hs, hr_sem,
+    psem, up_s, down_s, zr, fs, fr, ks, kr, js, jr, s1, r1, s2, r2,
+    qn_s, qn_r, qf_s, qf_r, gn_s, gn_r, gf_s, gf_r,
     ws1, wr1, ws2, wr2, ws3, wr3, ws4, wr4, fsem,
 ):
     row, col = lax.axis_index("row"), lax.axis_index("col")
@@ -64,10 +75,27 @@
     dcol, drow = hb * HD, hr * HD
     wr = W // nrow
     chunks = R // STEP
-    inner = 2 if ncol % 2 == 0 else 1
-    outer = ncol // inner
+    inner, outer, rin, rout = split(ncol) + split(nrow)
     a, b_in = col // inner, lax.rem(col, inner)
     flip = a * inner + inner - 1 - b_in
+    x_at, core = row // rin, lax.rem(row, rin)
+    twin = x_at * rin + rin - 1 - core
+    folded, half = folds(R, hb)
+    main_lanes = LANES if folded else R
+
+    def put_row(ref, b, s, n, x):
+        ref[b, s:s + 1, :] = x[:, :main_lanes]
+        if folded:
+            at = (s % 2) * half
+            ref[b, n + s // 2:n + s // 2 + 1, at:at + half] = x[:, main_lanes:]
+
+    def get_row(ref, b, s, n):
+        x = ref[b, s:s + 1, :]
+        if folded:
+            at = (s % 2) * half
+            tail = ref[b, n + s // 2:n + s // 2 + 1, at:at + half]
+            x = jnp.concatenate([x, tail], axis=1)
+        return x
 
     def load(t):
         rows = pl.ds(t * STEP, STEP)
@@ -85,21 +113,75 @@
     kv_all[row] = kv_own
     greet(nrow, ncol, row, col)
 
-    def relay(k):
-        src = lax.rem(a + outer - k, outer) * inner + b_in
-        return remote(qd_all.at[src], qd_all.at[src], fs.at[k], fr.at[k], row, flip)
-
-    first = []
-    for k in range(1, outer):
-        to = lax.rem(a + k, outer) * inner + b_in
-        first.append(remote(qd, qd_all.at[col], qs.at[k], qr.at[k], row, to))
+    def line(src):
+        return src * inner + b_in
+
+    def pass_up(src, ref):
+        return remote(ref, qd_all.at[line(src)], up_s.at[src], zr.at[src], row, col + inner)
+
+    def pass_down(src, ref):
+        return remote(ref, qd_all.at[line(src)], down_s.at[src], zr.at[src], row, col - inner)
+
+    def pass_flip(src, ref):
+        return remote(ref, qd_all.at[line(src)], fs.at[src], fr.at[src], row, flip)
+
+    @pl.when(a + 1 < outer)
+    def _():
+        pass_up(a, qd).start()
+
+    @pl.when(a > 0)
+    def _():
+        pass_down(a, qd).start()
+
     if inner == 2:
-        first.append(remote(qd, qd_all.at[col], fs.at[0], fr.at[0], row, flip))
-    for k in range(1, nrow):
-        to = lax.rem(row + k, nrow)
-        first.append(remote(kv, kv_all.at[row], ks.at[k], kr.at[k], to, col))
-    for copy in first:
-        copy.start()
+        pass_flip(a, qd).start()
+
+    def kv_far(k):
+        to = lax.rem(x_at + k, rout) * rin + core
+        return remote(kv, kv_all.at[row], ks.at[k], kr.at[k], to, col)
+
+    def kv_twin(k, ref):
+        src = lax.rem(x_at + rout - k, rout) * rin + core
+        return remote(ref, kv_all.at[src], js.at[k], jr.at[k], twin, col)
+
+    for k in range(1, rout):
+        kv_far(k).start()
+    if rin == 2:
+        kv_twin(0, kv).start()
+
+    def arrive(j):
+        @pl.when(a >= j)
+        def _():
+            src = a - j
+            here = qd_all.at[line(src)]
+            pass_up(src, here).wait_recv()
+
+            @pl.when(a + 1 < outer)
+            def _():
+                pass_up(src, here).start()
+
+            if inner == 2:
+                pass_flip(src, here).start()
+
+        @pl.when(a + j < outer)
+        def _():
+            src = a + j
+            here = qd_all.at[line(src)]
+            pass_down(src, here).wait_recv()
+
+            @pl.when(a > 0)
+            def _():
+                pass_down(src, here).start()
+
+            if inner == 2:
+                pass_flip(src, here).start()
+
+    def kv_arrive(k):
+        src = lax.rem(x_at + rout - k, rout) * rin + core
+        remote(kv, kv_all.at[src], ks.at[k], kr.at[k], row, col).wait_recv()
+        if rin == 2:
+            kv_twin(k, kv_all.at[src]).start()
+
     if Cp > C:
         pv[:, C:, :] = jnp.zeros((R, Cp - C, W), BF16)
 
@@ -111,18 +193,30 @@
             r = dot_nt(wt[...], pv[pl.ds(i, 2)].reshape(2 * Cp, W))
             bias[pl.ds(i, H, stride=R), :] = r[:, :Cp]
             bias[pl.ds(i + 1, H, stride=R), :] = r[:, Cp:]
-        for k in range(1, outer):
-
-            @pl.when(t == min(chunks - 1, chunks // 2 + 2 * (k - 1)))
+        for j in range(1, outer):
+            if HOP * j < chunks:
+
+                @pl.when(t == HOP * j)
+                def _():
+                    arrive(j)
+
+        if HOP < chunks:
+
+            @pl.when(t == HOP)
             def _():
-                src = lax.rem(a + outer - k, outer) * inner + b_in
-                remote(qd, qd_all.at[src], qs.at[k], qr.at[k], row, col).wait_recv()
-                if inner == 2:
-                    relay(k).start()
-
-    for k in range(1, nrow):
-        src = lax.rem(row + nrow - k, nrow)
-        remote(kv, kv_all.at[src], ks.at[k], kr.at[k], row, col).wait_recv()
+                for k in range(1, rout):
+                    kv_arrive(k)
+
+    if HOP >= chunks:
+        for k in range(1, rout):
+            kv_arrive(k)
+    for j in range(1, outer):
+        if HOP * j >= chunks:
+            arrive(j)
+    if rin == 2:
+        for k in range(rout):
+            src = lax.rem(x_at + rout - k, rout) * rin + rin - 1 - core
+            remote(kv, kv_all.at[src], js.at[k], jr.at[k], row, col).wait_recv()
 
     @pl.loop(0, nrow)
     def _(r):
@@ -130,11 +224,6 @@
         kt[pl.ds(r * hr, hr)] = x[:drow].reshape(hr, HD, C)
         vt[pl.ds(r * hr, hr)] = x[drow:].reshape(hr, HD, C)
 
-    if inner == 2:
-        for k in range(outer):
-            src = lax.rem(a + outer - k, outer) * inner + 1 - b_in
-            remote(qd, qd_all.at[src], fs.at[k], fr.at[k], row, col).wait_recv()
-
     lag = ncol // 2
 
     def combine():
@@ -142,19 +231,23 @@
             src = lax.rem(col + k, ncol)
             remote(st.at[src], got.at[src], s1.at[src], r1.at[src], row, col).wait_recv()
         got[col] = st[col]
-        top = got[0, 0]
-        for k in range(1, ncol):
-            top = jnp.maximum(top, got[k, 0])
-        total = jnp.zeros_like(top)
-        upper = jnp.zeros_like(top)
-        for k in range(ncol):
-            scale = jnp.exp(got[k, 0] - top)
-            total += got[k, 1] * scale
-            upper += got[k, 2] * scale
-        delta = upper / total
-        for k in range(ncol):
-            back[k, 0] = jnp.exp(got[k, 0] - top) / total
-            back[k, 1] = delta
+        sections = [(0, 0, hb)]
+        if folded:
+            sections.append((3 * hb, 2 * hb, hb // 2))
+        for lo, out, n in sections:
+            top = got[0, lo:lo + n]
+            for k in range(1, ncol):
+                top = jnp.maximum(top, got[k, lo:lo + n])
+            total = jnp.zeros_like(top)
+            upper = jnp.zeros_like(top)
+            for k in range(ncol):
+                scale = jnp.exp(got[k, lo:lo + n] - top)
+                total += got[k, lo + n:lo + 2 * n] * scale
+                upper += got[k, lo + 2 * n:lo + 3 * n] * scale
+            delta = upper / total
+            for k in range(ncol):
+                back[k, out:out + n] = jnp.exp(got[k, lo:lo + n] - top) / total
+                back[k, out + n:out + 2 * n] = delta
         bk[col] = back[col]
         for k in range(1, ncol):
             to = lax.rem(col + k, ncol)
@@ -162,6 +255,13 @@
 
     @pl.loop(0, ncol)
     def _(b):
+        if inner == 2:
+
+            @pl.when(lax.rem(b, inner) != b_in)
+            def _():
+                at = b // inner
+                remote(qd, qd_all.at[b], fs.at[at], fr.at[at], row, col).wait_recv()
+
         x = qd_all[b].T
         qt[pl.ds(b * hb, hb)] = (x[:dcol] * jnp.asarray(SCALE, BF16)).reshape(hb, HD, R)
         dt[pl.ds(b * hb, hb)] = x[dcol:].reshape(hb, HD, R)
@@ -181,9 +281,9 @@
             e = jnp.exp(s - top)
             e_buf[h] = e
             g_buf[h] = g
-            st[b, 0, pl.ds(t, 1)] = top
-            st[b, 1, pl.ds(t, 1)] = jnp.sum(e, axis=0, keepdims=True)
-            st[b, 2, pl.ds(t, 1)] = jnp.sum(e * g, axis=0, keepdims=True)
+            put_row(st, b, t, 3 * hb, top)
+            put_row(st, b, hb + t, 3 * hb, jnp.sum(e, axis=0, keepdims=True))
+            put_row(st, b, 2 * hb + t, 3 * hb, jnp.sum(e * g, axis=0, keepdims=True))
 
         @pl.when(col != b)
         def _():
@@ -196,7 +296,12 @@
     per = hr // hb if hr % hb == 0 else 0
 
     def send_dkv(r):
-        remote(dkv.at[r], dkv_got.at[row], gs.at[r], gr.at[row], r, col).start()
+        at = r // rin
+        return remote(dkv.at[r], dkv_near.at[at], gn_s.at[at], gn_r.at[at], twin, col)
+
+    def send_dq(b):
+        at = b // inner
+        return remote(dq.at[b], dq_near.at[at], qn_s.at[at], qn_r.at[at], row, flip)
 
     @pl.loop(0, ncol)
     def _(b):
@@ -211,36 +316,73 @@
         for t in range(hb):
             h = b * hb + t
             r = h // hr
-            w = e_buf[h] * bk[b, 0, pl.ds(t, 1)]
-            ds = (w * (g_buf[h] - bk[b, 1, pl.ds(t, 1)])).astype(BF16)
+            w = e_buf[h] * get_row(bk, b, t, 2 * hb)
+            ds = (w * (g_buf[h] - get_row(bk, b, hb + t, 2 * hb))).astype(BF16)
             low = w.astype(BF16)
-            dq[b, t] = (dot(kt[h], ds) * SCALE).astype(BF16)
+            y = (dot(kt[h], ds) * SCALE).astype(BF16)
+            dq[b, t * HD:(t + 1) * HD, :] = y[:, :main_lanes]
+            if folded:
+                lo, at = dcol + (t // 2) * HD, (t % 2) * half
+                dq[b, lo:lo + HD, at:at + half] = y[:, main_lanes:]
             dkv[r, 0, lax.rem(h, hr)] = dot_nt(qt[h], ds).astype(BF16)
             dkv[r, 1, lax.rem(h, hr)] = dot_nt(dt[h], low).astype(BF16)
             bias[pl.ds(pl.multiple_of(h * R, 8), R), pl.ds(0, C)] = ds.astype(F32).T
 
-        @pl.when(col != b)
-        def _():
-            remote(dq.at[b], dq_got.at[col], hs.at[b], hr_sem.at[col], row, b).start()
-
-        if per:
+        if inner == 2:
+
+            @pl.when(lax.rem(b, inner) != b_in)
+            def _():
+                send_dq(b).start()
+
+        if per and rin == 2:
             done = b // per
 
-            @pl.when(jnp.logical_and(lax.rem(b, per) == per - 1, row != done))
+            @pl.when(jnp.logical_and(lax.rem(b, per) == per - 1, lax.rem(done, rin) != core))
             def _():
-                send_dkv(done)
-
-    if not per:
-        for k in range(1, nrow):
-            send_dkv(lax.rem(row + k, nrow))
+                send_dkv(done).start()
+
+    if not per and rin == 2:
+        for x in range(rout):
+            send_dkv(x * rin + rin - 1 - core).start()
+
+    def merge_dq(at):
+        value = dq[at * inner + b_in].astype(F32)
+        if inner == 2:
+            remote(dq.at[0], dq_near.at[at], qn_s.at[0], qn_r.at[at], row, col).wait_recv()
+            value += dq_near[at].astype(F32)
+        return value
+
+    def merge_dkv(at):
+        value = dkv[at * rin + core].astype(F32)
+        if rin == 2:
+            remote(dkv.at[0], dkv_near.at[at], gn_s.at[0], gn_r.at[at], row, col).wait_recv()
+            value += dkv_near[at].astype(F32)
+        return value
+
+    def far_dq(at):
+        to = at * inner + b_in
+        return remote(dq.at[to], dq_far.at[a], qf_s.at[at], qf_r.at[a], row, to)
+
+    def far_dkv(at):
+        to = at * rin + core
+        return remote(dkv.at[to], dkv_far.at[x_at], gf_s.at[at], gf_r.at[x_at], to, col)
+
+    def merge():
+        for k in range(1, outer):
+            at = lax.rem(a + k, outer)
+            dq[at * inner + b_in] = merge_dq(at).astype(BF16)
+            far_dq(at).start()
+        for k in range(1, rout):
+            at = lax.rem(x_at + k, rout)
+            dkv[at * rin + core] = merge_dkv(at).astype(BF16)
+            far_dkv(at).start()
 
     acc[...] = jnp.zeros_like(acc)
 
     def rows_of(i):
         return bias[pl.ds(i, H, stride=R), :]
 
-    @pl.loop(0, chunks)
-    def _(t):
+    def weight(t):
         total = acc[...]
         for u in range(0, STEP, 2):
             i = t * STEP + u
@@ -250,9 +392,13 @@
             total = total + dot(lhs, pv[pl.ds(i, 2)].reshape(2 * Cp, W))
         acc[...] = total
 
+    pl.loop(0, chunks // 2)(weight)
+    merge()
+    pl.loop(chunks // 2, chunks)(weight)
+
     for r in range(nrow):
         for b in range(ncol):
-            wb[r, b] = acc[b * hb:(b + 1) * hb, r * wr:(r + 1) * wr]
+            wb[r, b] = acc[b * hb:(b + 1) * hb, r * wr:(r + 1) * wr].astype(BF16)
 
     def put(t, slot):
         return pltpu.make_async_copy(
@@ -278,10 +424,10 @@
         to = lax.rem(row + k, nrow)
         remote(wb.at[to], w1.at[k], ws1.at[k], wr1.at[k], to, col).start()
     flat(cuts[0], cuts[1])
-    total = wb[row]
+    total = wb[row].astype(F32)
     for k in range(1, nrow):
         remote(wb.at[0], w1.at[k], ws1.at[k], wr1.at[k], row, col).wait_recv()
-        total += w1[k]
+        total += w1[k].astype(F32)
     w1sum[...] = total
     for k in range(1, ncol):
         to = lax.rem(col + k, ncol)
@@ -298,19 +444,25 @@
         remote(w2sum, wb_out.at[row, col], ws3.at[k], wr3.at[k], row, to).start()
     flat(cuts[2], cuts[3])
 
-    grad = dkv[row].astype(F32)
-    for k in range(1, nrow):
-        src = lax.rem(row + k, nrow)
-        remote(dkv.at[0], dkv_got.at[src], gs.at[0], gr.at[src], row, col).wait_recv()
-        grad += dkv_got[src].astype(F32)
+    grad = merge_dkv(x_at)
+    for k in range(1, rout):
+        src = lax.rem(x_at + k, rout)
+        remote(dkv.at[0], dkv_far.at[src], gf_s.at[0], gf_r.at[src], row, col).wait_recv()
+        grad += dkv_far[src].astype(F32)
     k_out[...] = grad[0].reshape(drow, C).T.astype(BF16)
     v_out[...] = grad[1].reshape(drow, C).T.astype(BF16)
-    total_q = dq[col].astype(F32)
-    for k in range(1, ncol):
-        src = lax.rem(col + k, ncol)
-        remote(dq.at[0], dq_got.at[src], hs.at[0], hr_sem.at[src], row, col).wait_recv()
-        total_q += dq_got[src].astype(F32)
-    q_out[...] = total_q.reshape(dcol, R).T.astype(BF16)
+    grad = merge_dq(a)
+    for k in range(1, outer):
+        src = lax.rem(a + k, outer)
+        remote(dq.at[0], dq_far.at[src], qf_s.at[0], qf_r.at[src], row, col).wait_recv()
+        grad += dq_far[src].astype(F32)
+    if folded:
+        tail = grad[dcol:].reshape(hb // 2, HD, LANES)
+        tail = jnp.stack([tail[:, :, :half], tail[:, :, half:]], axis=1).reshape(dcol, half)
+        q_out[:LANES] = grad[:dcol].T.astype(BF16)
+        q_out[LANES:] = tail.T.astype(BF16)
+    else:
+        q_out[...] = grad.T.astype(BF16)
 
     for k in range(1, ncol):
         src = lax.rem(col + ncol - k, ncol)
@@ -325,21 +477,36 @@
 
     for t in range(max(0, chunks - SLOTS), chunks):
         put(t, t % SLOTS).wait()
-    for copy in first:
-        copy.wait_send()
-    if inner == 2:
-        for k in range(1, outer):
-            relay(k).wait_send()
+    for src in range(outer):
+
+        @pl.when(jnp.logical_and(a >= src, a + 1 < outer))
+        def _():
+            pass_up(src, qd).wait_send()
+
+        @pl.when(jnp.logical_and(a <= src, a > 0))
+        def _():
+            pass_down(src, qd).wait_send()
+
+        if inner == 2:
+            pass_flip(src, qd).wait_send()
+            send_dq(src * inner + 1 - b_in).wait_send()
+    for k in range(rout):
+        if rin == 2:
+            kv_twin(k, kv).wait_send()
+            send_dkv(k * rin + 1 - core).wait_send()
+        if k:
+            kv_far(k).wait_send()
+            far_dkv(lax.rem(x_at + k, rout)).wait_send()
+    for k in range(1, outer):
+        far_dq(lax.rem(a + k, outer)).wait_send()
     for k in range(1, ncol):
         to = lax.rem(col + k, ncol)
         remote(st.at[to], got.at[col], s1.at[to], r1.at[col], row, to).wait_send()
         remote(back.at[to], bk.at[col], s2.at[to], r2.at[col], row, to).wait_send()
-        remote(dq.at[to], dq_got.at[col], hs.at[to], hr_sem.at[col], row, to).wait_send()
         remote(w1sum.at[to], w2.at[k], ws2.at[k], wr2.at[k], row, to).wait_send()
         remote(w2sum, wb_out.at[row, col], ws3.at[k], wr3.at[k], row, to).wait_send()
     for k in range(1, nrow):
         to = lax.rem(row + k, nrow)
-        remote(dkv.at[to], dkv_got.at[row], gs.at[to], gr.at[row], to, col).wait_send()
         remote(wb.at[to], w1.at[k], ws1.at[k], wr1.at[k], to, col).wait_send()
         remote(wb_out.at[row], wb_out.at[row], ws4.at[k], wr4.at[k], to, col).wait_send()
 
@@ -352,6 +519,11 @@
     Cp = -(-C // LANES) * LANES
     wr = W // nrow
     shape = jax.ShapeDtypeStruct
+    (inner, outer), (rin, rout) = split(ncol), split(nrow)
+    folded, _ = folds(R, hb)
+    width = LANES if folded else R
+    extra = 3 * hb // 2 if folded else 0
+    dq_rows = dcol + (dcol // 2 if folded else 0)
     return pl.pallas_call(
         functools.partial(main_kernel, nrow, ncol),
         out_shape=(
@@ -377,26 +549,29 @@
             VMEM((H, HD, R), BF16),
             VMEM((H, HD, C), BF16),
             VMEM((H, HD, C), BF16),
-            VMEM((ncol, 3, hb, R), F32),
-            VMEM((ncol, 3, hb, R), F32),
-            VMEM((ncol, 2, hb, R), F32),
-            VMEM((ncol, 2, hb, R), F32),
-            VMEM((ncol, hb, HD, R), BF16),
-            VMEM((ncol, hb, HD, R), BF16),
+            VMEM((ncol, 3 * hb + extra, width), F32),
+            VMEM((ncol, 3 * hb + extra, width), F32),
+            VMEM((ncol, 2 * hb + (hb if folded else 0), width), F32),
+            VMEM((ncol, 2 * hb + (hb if folded else 0), width), F32),
+            VMEM((ncol, dq_rows, width), BF16),
+            VMEM((outer, dq_rows, width), BF16),
+            VMEM((outer, dq_rows, width), BF16),
             VMEM((nrow, 2, hr, HD, C), BF16),
-            VMEM((nrow, 2, hr, HD, C), BF16),
+            VMEM((rout, 2, hr, HD, C), BF16),
+            VMEM((rout, 2, hr, HD, C), BF16),
             VMEM((H, W), F32),
-            VMEM((nrow, ncol, hb, wr), F32),
-            VMEM((nrow, ncol, hb, wr), F32),
+            VMEM((nrow, ncol, hb, wr), BF16),
+            VMEM((nrow, ncol, hb, wr), BF16),
             VMEM((ncol, hb, wr), F32),
             VMEM((ncol, hb, wr), F32),
             VMEM((hb, wr), F32),
             VMEM((SLOTS, STEP, C, H), BF16),
             DMA((R // STEP,)),
+            DMA((outer,)), DMA((outer,)), DMA((outer,)), DMA((outer,)), DMA((outer,)),
+            DMA((rout,)), DMA((rout,)), DMA((rout,)), DMA((rout,)),
             DMA((ncol,)), DMA((ncol,)), DMA((ncol,)), DMA((ncol,)),
-            DMA((nrow,)), DMA((nrow,)),
-            DMA((ncol,)), DMA((ncol,)), DMA((ncol,)), DMA((ncol,)),
-            DMA((nrow,)), DMA((nrow,)), DMA((ncol,)), DMA((ncol,)),
+            DMA((outer,)), DMA((outer,)), DMA((outer,)), DMA((outer,)),
+            DMA((rout,)), DMA((rout,)), DMA((rout,)), DMA((rout,)),
             DMA((nrow,)), DMA((nrow,)), DMA((ncol,)), DMA((ncol,)),
             DMA((ncol,)), DMA((ncol,)), DMA((nrow,)), DMA((nrow,)),
             DMA((SLOTS,)),
@@ -421,8 +596,9 @@
             wo[:, r * wr:(r + 1) * wr] = wb[r].reshape(H, wr)
 
 
-def finish(f, wt, wb, q, k, v, block=16):
+def finish(f, wt, wb, q, k, v):
     R, C, H = f.shape
+    block = 3 * STEP if R % (3 * STEP) == 0 else STEP
     W = wt.shape[1]
 
     def whole(x):

time: 96.8 us -> 78 us (0.81)
  Pallas kernels: 95.7 us -> 77.1 us
    pallas_call x1, Pallas kernels: 81.8 us -> 66.4 us  [main(): pl.pallas_call(functools.partial(main_kernel, nrow, ncol), out_shape=(sha...]
    pallas_call x1, Pallas kernels: 13.9 us -> 10.7 us  [finish(): pl.pallas_call(finish_kernel, grid=(R // block,), out_shape=(jax.ShapeDty...]
where the time goes in v2:
time: 78 us; the launch traced here: 77.7 us
  Pallas kernels  77.1 us (99%)
    pallas_call x1, Pallas kernels, main(): pl.pallas_call(functools.partial(main_kernel, nrow, ncol), out_shape=(sha...  66.4 us
    pallas_call x1, Pallas kernels, finish(): pl.pallas_call(finish_kernel, grid=(R // block,), out_shape=(jax.ShapeDty...  10.7 us

profile of v2, /device:TPU:0, one launch (start us, length us, event | category | flops | bytes accessed | tf_op | source)
XLA Modules:
  0.0 77.7 jit_solution(5230872528402336750)
XLA Ops:
  0.6 66.4 %shard_map.101 = (bf16[192,96,96]{2,1,0:T(8,128)(2,1)}, f32[4,8,12,128]{3,2,1,0:T(8,128)}, bf16[192,192]{1,0:T(8,128)(2,1)}, bf16[96,384]{1,0:T(8,128)(2,1)}, bf16[96,384]{1,0:T(8,128)(2,1)}) custom-call(bf16[96,512]{1,0:T(8,128)(2,1)} %bitcast.2, bf16[192,96,512]{2,1,0:T(8,128)(2,1)} %pair.1, bf16[192,192]{1,0:T(8,128)(2,1)} %q.1, bf16[96,384]{1,0:T(8,128)(2,1)} %k_in.1, ...), custom_call_target="tpu_custom_call" | custom-call | tf_op jit(solution)/shard_map/pallas_call | solution.py:527
  67.1 10.7 %shard_map.102 = (bf16[192,96,512]{2,1,0:T(8,128)(2,1)}, f32[96,512]{1,0:T(8,128)}, bf16[192,192]{1,0:T(8,128)(2,1)}, bf16[96,384]{1,0:T(8,128)(2,1)}, bf16[96,384]{1,0:T(8,128)(2,1)}) custom-call(bf16[192,96,96]{2,1,0:T(8,128)(2,1)} %get-tuple-element.15.f, bf16[96,512]{1,0:T(8,128)(2,1)} %bitcast.3, f32[4,8,12,128]{3,2,1,0:T(8,128)} %get-tuple-element.16.wb, ...), custom_call_target="tpu_custom_call" | custom-call | tf_op jit(solution)/shard_map/pallas_call | solution.py:607

commit v3 on v2

--- a/solution.py
+++ b/solution.py
@@ -80,6 +80,15 @@
     flip = a * inner + inner - 1 - b_in
     x_at, core = row // rin, lax.rem(row, rin)
     twin = x_at * rin + rin - 1 - core
+    upper_half = (2 * a) // outer
+    slot = b_in * outer + (1 - upper_half) * 2 * a + upper_half * (2 * (outer - a) - 1)
+
+    def block_at(p):
+        q = lax.rem(p, outer)
+        odd = lax.rem(q, 2)
+        end = (1 - odd) * (q // 2) + odd * (outer - 1 - q // 2)
+        return end * inner + p // outer
+
     folded, half = folds(R, hb)
     main_lanes = LANES if folded else R
 
@@ -254,7 +263,8 @@
             remote(back.at[to], bk.at[col], s2.at[to], r2.at[col], row, to).start()
 
     @pl.loop(0, ncol)
-    def _(b):
+    def _(p):
+        b = block_at(p)
         if inner == 2:
 
             @pl.when(lax.rem(b, inner) != b_in)
@@ -289,11 +299,9 @@
         def _():
             remote(st.at[b], got.at[col], s1.at[b], r1.at[col], row, b).start()
 
-        @pl.when(col == b - lag)
+        @pl.when(slot == p - lag)
         def _():
             combine()
-
-    per = hr // hb if hr % hb == 0 else 0
 
     def send_dkv(r):
         at = r // rin
@@ -304,8 +312,10 @@
         return remote(dq.at[b], dq_near.at[at], qn_s.at[at], qn_r.at[at], row, flip)
 
     @pl.loop(0, ncol)
-    def _(b):
-        @pl.when(col == ncol - lag + b)
+    def _(p):
+        b = block_at(p)
+
+        @pl.when(slot == ncol - lag + p)
         def _():
             combine()
 
@@ -334,14 +344,7 @@
             def _():
                 send_dq(b).start()
 
-        if per and rin == 2:
-            done = b // per
-
-            @pl.when(jnp.logical_and(lax.rem(b, per) == per - 1, lax.rem(done, rin) != core))
-            def _():
-                send_dkv(done).start()
-
-    if not per and rin == 2:
+    if rin == 2:
         for x in range(rout):
             send_dkv(x * rin + rin - 1 - core).start()
 
@@ -382,19 +385,22 @@
     def rows_of(i):
         return bias[pl.ds(i, H, stride=R), :]
 
+    wide = 2 * STEP if R % (4 * STEP) == 0 else STEP
+    laps = R // wide
+
     def weight(t):
         total = acc[...]
-        for u in range(0, STEP, 2):
-            i = t * STEP + u
+        for u in range(0, wide, 2):
+            i = t * wide + u
             lhs = jnp.concatenate(
                 [rows_of(i).astype(BF16), rows_of(i + 1).astype(BF16)], axis=1
             )
             total = total + dot(lhs, pv[pl.ds(i, 2)].reshape(2 * Cp, W))
         acc[...] = total
 
-    pl.loop(0, chunks // 2)(weight)
+    pl.loop(0, laps // 2)(weight)
     merge()
-    pl.loop(chunks // 2, chunks)(weight)
+    pl.loop(laps // 2, laps)(weight)
 
     for r in range(nrow):
         for b in range(ncol):
@@ -437,6 +443,7 @@
     for k in range(1, ncol):
         remote(w1sum.at[0], w2.at[k], ws2.at[k], wr2.at[k], row, col).wait_recv()
         part += w2[k]
+    part = part.astype(BF16)
     w2sum[...] = part
     wb_out[row, col] = part
     for k in range(1, ncol):
@@ -528,7 +535,7 @@
         functools.partial(main_kernel, nrow, ncol),
         out_shape=(
             shape((R, C, H), BF16),
-            shape((nrow, ncol, hb, wr), F32),
+            shape((nrow, ncol, hb, wr), BF16),
             shape((R, dcol), BF16),
             shape((C, drow), BF16),
             shape((C, drow), BF16),
@@ -564,7 +571,7 @@
             VMEM((nrow, ncol, hb, wr), BF16),
             VMEM((ncol, hb, wr), F32),
             VMEM((ncol, hb, wr), F32),
-            VMEM((hb, wr), F32),
+            VMEM((hb, wr), BF16),
             VMEM((SLOTS, STEP, C, H), BF16),
             DMA((R // STEP,)),
             DMA((outer,)), DMA((outer,)), DMA((outer,)), DMA((outer,)), DMA((outer,)),
@@ -593,7 +600,7 @@
         vo[...] = v[...]
         nrow, wr = wb.shape[0], wb.shape[3]
         for r in range(nrow):
-            wo[:, r * wr:(r + 1) * wr] = wb[r].reshape(H, wr)
+            wo[:, r * wr:(r + 1) * wr] = wb[r].astype(F32).reshape(H, wr)
 
 
 def finish(f, wt, wb, q, k, v):

time: 78 us -> 77.1 us (0.988)
  Pallas kernels: 77.1 us -> 76.2 us
    pallas_call x1, Pallas kernels: 66.4 us -> 65.6 us  [main(): pl.pallas_call(functools.partial(main_kernel, nrow, ncol), out_shape=(sha...]
where the time goes in v3:
time: 77.1 us; the launch traced here: 76.8 us
  Pallas kernels  76.2 us (99%)
    pallas_call x1, Pallas kernels, main(): pl.pallas_call(functools.partial(main_kernel, nrow, ncol), out_shape=(sha...  65.6 us
    pallas_call x1, Pallas kernels, finish(): pl.pallas_call(finish_kernel, grid=(R // block,), out_shape=(jax.ShapeDty...  10.7 us

profile of v3, /device:TPU:0, one launch (start us, length us, event | category | flops | bytes accessed | tf_op | source)
XLA Modules:
  0.0 76.8 jit_solution(17633119101360161058)
XLA Ops:
  0.6 65.6 %shard_map.101 = (bf16[192,96,96]{2,1,0:T(8,128)(2,1)}, bf16[4,8,12,128]{3,2,1,0:T(8,128)(2,1)}, bf16[192,192]{1,0:T(8,128)(2,1)}, bf16[96,384]{1,0:T(8,128)(2,1)}, bf16[96,384]{1,0:T(8,128)(2,1)}) custom-call(bf16[96,512]{1,0:T(8,128)(2,1)} %bitcast.2, bf16[192,96,512]{2,1,0:T(8,128)(2,1)} %pair.1, bf16[192,192]{1,0:T(8,128)(2,1)} %q.1, ...), custom_call_target="tpu_custom_call" | custom-call | tf_op jit(solution)/shard_map/pallas_call | solution.py:534
  66.2 10.7 %shard_map.102 = (bf16[192,96,512]{2,1,0:T(8,128)(2,1)}, f32[96,512]{1,0:T(8,128)}, bf16[192,192]{1,0:T(8,128)(2,1)}, bf16[96,384]{1,0:T(8,128)(2,1)}, bf16[96,384]{1,0:T(8,128)(2,1)}) custom-call(bf16[192,96,96]{2,1,0:T(8,128)(2,1)} %get-tuple-element.15.f, bf16[96,512]{1,0:T(8,128)(2,1)} %bitcast.3, bf16[4,8,12,128]{3,2,1,0:T(8,128)(2,1)} %get-tuple-element.16.wb, ...), custom_call_target="tpu_custom_call" | custom-call | tf_op jit(solution)/shard_map/pallas_call | solution.py:614

commit v4 on v3

--- a/solution.py
+++ b/solution.py
@@ -205,7 +205,7 @@
         for j in range(1, outer):
             if HOP * j < chunks:
 
-                @pl.when(t == HOP * j)
+                @pl.when(t == HOP * j - 1)
                 def _():
                     arrive(j)
 
@@ -589,31 +589,61 @@
     )(wt, pair, q, k, v, d)
 
 
-def finish_kernel(f, wt, wb, q, k, v, d_pair, wo, qo, ko, vo):
-    rows, C, H = f.shape
-    d_pair[...] = dot(f[...].reshape(rows * C, H), wt[...]).astype(BF16).reshape(d_pair.shape)
-
-    @pl.when(pl.program_id(0) == 0)
-    def _():
-        qo[...] = q[...]
-        ko[...] = k[...]
-        vo[...] = v[...]
-        nrow, wr = wb.shape[0], wb.shape[3]
-        for r in range(nrow):
-            wo[:, r * wr:(r + 1) * wr] = wb[r].astype(F32).reshape(H, wr)
+def finish_kernel(
+    f, wt, wb, q, k, v, d_pair, wo, qo, ko, vo, f_all, stage, w_all, fsem, osem, ssem
+):
+    R, C, H = f.shape
+    laps = R // STEP
+    slots = stage.shape[0]
+
+    def fetch(t):
+        rows = pl.ds(t * STEP, STEP)
+        return pltpu.make_async_copy(f.at[rows], f_all.at[rows], fsem.at[t])
+
+    def put(t, slot):
+        rows = pl.ds(t * STEP, STEP)
+        return pltpu.make_async_copy(stage.at[slot], d_pair.at[rows], osem.at[slot])
+
+    @pl.loop(0, laps)
+    def _(t):
+        fetch(t).start()
+
+    nrow, wr = wb.shape[0], wb.shape[3]
+    for r in range(nrow):
+        w_all[:, r * wr:(r + 1) * wr] = wb[r].astype(F32).reshape(H, wr)
+    small = [
+        pltpu.make_async_copy(src, dst, ssem.at[n])
+        for n, (src, dst) in enumerate([(w_all, wo), (q, qo), (k, ko), (v, vo)])
+    ]
+    for copy in small:
+        copy.start()
+
+    @pl.loop(0, laps)
+    def _(t):
+        slot = lax.rem(t, slots)
+        fetch(t).wait()
+
+        @pl.when(t >= slots)
+        def _():
+            put(t - slots, slot).wait()
+
+        lhs = f_all[pl.ds(t * STEP, STEP)].reshape(STEP * C, H)
+        stage[slot] = dot(lhs, wt[...]).astype(BF16).reshape(STEP, C, stage.shape[3])
+        put(t, slot).start()
+
+    for t in range(max(0, laps - slots), laps):
+        put(t, t % slots).wait()
+    for copy in small:
+        copy.wait()
 
 
 def finish(f, wt, wb, q, k, v):
     R, C, H = f.shape
-    block = 3 * STEP if R % (3 * STEP) == 0 else STEP
     W = wt.shape[1]
-
-    def whole(x):
-        return pl.BlockSpec(x.shape, lambda i: (0,) * len(x.shape))
-
+    laps = R // STEP
+    slots = min(4, laps)
     return pl.pallas_call(
         finish_kernel,
-        grid=(R // block,),
         out_shape=(
             jax.ShapeDtypeStruct((R, C, W), BF16),
             jax.ShapeDtypeStruct((H, W), F32),
@@ -621,13 +651,17 @@
             jax.ShapeDtypeStruct(k.shape, BF16),
             jax.ShapeDtypeStruct(v.shape, BF16),
         ),
-        in_specs=[pl.BlockSpec((block, C, H), lambda i: (i, 0, 0))]
-        + [whole(x) for x in (wt, wb, q, k, v)],
-        out_specs=(
-            pl.BlockSpec((block, C, W), lambda i: (i, 0, 0)),
-            pl.BlockSpec((H, W), lambda i: (0, 0)),
-            whole(q), whole(k), whole(v),
-        ),
+        in_specs=[pl.BlockSpec(memory_space=pl.ANY)] + [pl.BlockSpec(memory_space=VMEM)] * 5,
+        out_specs=[pl.BlockSpec(memory_space=pl.ANY)] * 5,
+        scratch_shapes=[
+            VMEM((R, C, H), BF16),
+            VMEM((slots, STEP, C, W), BF16),
+            VMEM((H, W), F32),
+            DMA((laps,)),
+            DMA((slots,)),
+            DMA((4,)),
+        ],
+        compiler_params=pltpu.CompilerParams(vmem_limit_bytes=67043328),
     )(f, wt, wb, q, k, v)
 
 

time: 77.1 us -> 75.7 us (0.982)
  Pallas kernels: 76.2 us -> 74.9 us
    pallas_call x1, Pallas kernels: 65.6 us -> 64.7 us  [main(): pl.pallas_call(functools.partial(main_kernel, nrow, ncol), out_shape=(sha...]
where the time goes in v4:
time: 75.7 us; the launch traced here: 75.5 us
  Pallas kernels  74.9 us (99%)
    pallas_call x1, Pallas kernels, main(): pl.pallas_call(functools.partial(main_kernel, nrow, ncol), out_shape=(sha...  64.7 us
    pallas_call x1, Pallas kernels, finish(): pl.pallas_call(finish_kernel, out_shape=(jax.ShapeDtypeStruct((R, C, W),...  10.2 us

profile of v4, /device:TPU:0, one launch (start us, length us, event | category | flops | bytes accessed | tf_op | source)
XLA Modules:
  0.0 75.5 jit_solution(17185097824019193132)
XLA Ops:
  0.6 64.7 %shard_map.101 = (bf16[192,96,96]{2,1,0:T(8,128)(2,1)}, bf16[4,8,12,128]{3,2,1,0:T(8,128)(2,1)}, bf16[192,192]{1,0:T(8,128)(2,1)}, bf16[96,384]{1,0:T(8,128)(2,1)}, bf16[96,384]{1,0:T(8,128)(2,1)}) custom-call(bf16[96,512]{1,0:T(8,128)(2,1)} %bitcast.2, bf16[192,96,512]{2,1,0:T(8,128)(2,1)} %pair.1, bf16[192,192]{1,0:T(8,128)(2,1)} %q.1, ...), custom_call_target="tpu_custom_call" | custom-call | tf_op jit(solution)/shard_map/pallas_call | solution.py:534
  65.4 10.2 %shard_map.102 = (bf16[192,96,512]{2,1,0:T(8,128)(2,1)}, f32[96,512]{1,0:T(8,128)}, bf16[192,192]{1,0:T(8,128)(2,1)}, bf16[96,384]{1,0:T(8,128)(2,1)}, bf16[96,384]{1,0:T(8,128)(2,1)}) custom-call(bf16[192,96,96]{2,1,0:T(8,128)(2,1)} %get-tuple-element.15.f, bf16[96,512]{1,0:T(8,128)(2,1)} %bitcast.3, bf16[4,8,12,128]{3,2,1,0:T(8,128)(2,1)} %get-tuple-element.16.wb, ...), custom_call_target="tpu_custom_call" | custom-call | tf_op jit(solution)/shard_map/pallas_call | solution.py:645

commit v5 on v4

--- a/solution.py
+++ b/solution.py
@@ -233,7 +233,7 @@
         kt[pl.ds(r * hr, hr)] = x[:drow].reshape(hr, HD, C)
         vt[pl.ds(r * hr, hr)] = x[drow:].reshape(hr, HD, C)
 
-    lag = ncol // 2
+    lag = min(ncol - 1, ncol // 2 + 1)
 
     def combine():
         for k in range(1, ncol):

time: 75.7 us -> 76.4 us (level)
  no operation moved by 1% of the time
where the time goes in v5:
time: 76.4 us; the launch traced here: 76.2 us
  Pallas kernels  75.6 us (99%)
    pallas_call x1, Pallas kernels, main(): pl.pallas_call(functools.partial(main_kernel, nrow, ncol), out_shape=(sha...  65.4 us
    pallas_call x1, Pallas kernels, finish(): pl.pallas_call(finish_kernel, out_shape=(jax.ShapeDtypeStruct((R, C, W),...  10.2 us

profile of v5, /device:TPU:0, one launch (start us, length us, event | category | flops | bytes accessed | tf_op | source)
XLA Modules:
  0.0 76.2 jit_solution(1394306118185589466)
XLA Ops:
  0.6 65.4 %shard_map.101 = (bf16[192,96,96]{2,1,0:T(8,128)(2,1)}, bf16[4,8,12,128]{3,2,1,0:T(8,128)(2,1)}, bf16[192,192]{1,0:T(8,128)(2,1)}, bf16[96,384]{1,0:T(8,128)(2,1)}, bf16[96,384]{1,0:T(8,128)(2,1)}) custom-call(bf16[96,512]{1,0:T(8,128)(2,1)} %bitcast.2, bf16[192,96,512]{2,1,0:T(8,128)(2,1)} %pair.1, bf16[192,192]{1,0:T(8,128)(2,1)} %q.1, ...), custom_call_target="tpu_custom_call" | custom-call | tf_op jit(solution)/shard_map/pallas_call | solution.py:534
  66.1 10.2 %shard_map.102 = (bf16[192,96,512]{2,1,0:T(8,128)(2,1)}, f32[96,512]{1,0:T(8,128)}, bf16[192,192]{1,0:T(8,128)(2,1)}, bf16[96,384]{1,0:T(8,128)(2,1)}, bf16[96,384]{1,0:T(8,128)(2,1)}) custom-call(bf16[192,96,96]{2,1,0:T(8,128)(2,1)} %get-tuple-element.15.f, bf16[96,512]{1,0:T(8,128)(2,1)} %bitcast.3, bf16[4,8,12,128]{3,2,1,0:T(8,128)(2,1)} %get-tuple-element.16.wb, ...), custom_call_target="tpu_custom_call" | custom-call | tf_op jit(solution)/shard_map/pallas_call | solution.py:645
